TPU v7x, 512 devices: a whole 4x4x16 slice. The times are simulated.
512 devices in a mesh: dp: 64 (over z, x), seq: 8 (over y, core).
Axes of the slice: x: 4, y: 4, z: 16, core: 2. Of those that a mesh axis runs over, the one named last changes fastest.
Arguments:
- acts: bfloat16 [65536, 4096], P('dp', 'seq'), may hold values from -6 to 6
- upstream: bfloat16 [65536, 1024], P(('dp', 'seq')), may hold values from -0.005859375 to 0.005859375
- keep_lists: int32 [64, 8], replicated, may hold values from 0 to 15, all different within a row
- left_gram: float32 [8, 64, 1, 64, 64], P('seq', 'dp'), as said below
- right_gram: float32 [8, 64, 1, 64, 64], P('seq', 'dp'), as said below
- left_basis: float32 [8, 64, 1, 64, 64], P('seq', 'dp'), may hold values from -0.75 to 0.75
- right_basis: float32 [8, 64, 1, 64, 64], P('seq', 'dp'), may hold values from -0.75 to 0.75
- second_moment: float32 [8, 64, 1, 64, 64], P('seq', 'dp'), may hold values from 0.004 to 0.04
Outputs:
- new_left: float32 [8, 64, 1, 64, 64], P('seq', 'dp')
- new_right: float32 [8, 64, 1, 64, 64], P('seq', 'dp')
- direction: float32 [8, 64, 1, 64, 64], P('seq', 'dp')
Inputs may be any that keep to these rules, and one draw needn't show every extreme that they name: `keep_lists`: each row lists 8 different column blocks, and every column block is kept in some row. `left_gram`: each block is symmetric. `right_gram`: each block is symmetric.
All inputs are finite; a program needn't handle non-finite values.
Results may differ from a plain program's by a relative error of at most 0.0003.
Values may be sent and summed in bfloat16 or wider, within the bound.
No kernel may reach another device: no remote copies, remote signals or barrier semaphores. Data moves between devices by JAX's collectives and lax.ppermute only.
A program may use at most 64 MiB of HBM per device.

v0:
```python
import jax
import jax.numpy as jnp
from jax import lax
from jax.sharding import PartitionSpec as P

BLOCK = 64


def precondition(gradient, left_gram, right_gram, left_basis, right_basis, second_moment):
    highest = lax.Precision.HIGHEST
    new_left = 0.95 * left_gram + 0.05 * jnp.einsum(
        "...ij,...kj->...ik", gradient, gradient, precision=highest
    )
    new_right = 0.95 * right_gram + 0.05 * jnp.einsum(
        "...ji,...jk->...ik", gradient, gradient, precision=highest
    )
    partial_rot = jnp.einsum("...ji,...jk->...ik", left_basis, gradient, precision=highest)
    rotated = jnp.einsum("...ij,...jk->...ik", partial_rot, right_basis, precision=highest)
    second = 0.95 * second_moment + 0.05 * rotated * rotated
    scaled = rotated / (jnp.sqrt(second) + 1e-08)
    partial_back = jnp.einsum("...ij,...jk->...ik", left_basis, scaled, precision=highest)
    direction = jnp.einsum("...ij,...kj->...ik", partial_back, right_basis, precision=highest)
    return (new_left, new_right, direction)


def per_device(
    acts, upstream, keep_lists, left_gram, right_gram, left_basis, right_basis, second_moment
):
    share_rows = acts.shape[1]
    share_blocks = share_rows // BLOCK
    kept_share = lax.dynamic_slice_in_dim(
        keep_lists, lax.axis_index("seq") * share_blocks, share_blocks, 0
    )
    gathered = lax.all_gather(upstream, "seq", axis=0, tiled=True)
    grad = lax.dot_general(
        acts, gathered, (((0,), (0,)), ((), ())), preferred_element_type=jnp.float32
    )
    tiles = grad.reshape(share_blocks, BLOCK, grad.shape[1] // BLOCK, BLOCK)
    picked = jnp.take_along_axis(tiles, kept_share[:, None, :, None], axis=2)
    packed = picked.transpose(0, 2, 1, 3)
    data_size = lax.axis_size("dp")
    outgoing = packed.reshape(data_size, -1, BLOCK * BLOCK)
    arrived = lax.all_to_all(outgoing, "dp", split_axis=0, concat_axis=0, tiled=True)
    owned_sum = jnp.sum(arrived, axis=0)
    gradient = owned_sum.reshape(1, 1, -1, BLOCK, BLOCK)
    new_left, new_right, direction = precondition(
        gradient, left_gram, right_gram, left_basis, right_basis, second_moment
    )
    return (new_left, new_right, direction)


def solution(mesh):
    in_specs = (
        P("dp", "seq"),
        P(("dp", "seq"), None),
        P(),
        P("seq", "dp", None, None, None),
        P("seq", "dp", None, None, None),
        P("seq", "dp", None, None, None),
        P("seq", "dp", None, None, None),
        P("seq", "dp", None, None, None),
    )
    out_specs = (
        P("seq", "dp", None, None, None),
        P("seq", "dp", None, None, None),
        P("seq", "dp", None, None, None),
    )
    return jax.shard_map(
        per_device, mesh=mesh, in_specs=in_specs, out_specs=out_specs, check_vma=False
    )
```

profile of v0, /device:TPU:6, one launch (start us, length us, event | category | flops | bytes accessed | tf_op | source)
XLA Modules:
  0.0 149.2 jit_solution(2693960995745928037)
XLA Ops:
  7.2 0.0 copy-start
  7.2 0.0 all-gather.2.cloned.1.call-start
  7.2 0.7 all-gather.2.cloned.1.call-update
  7.9 0.8 constant_dynamic-slice_fusion
  8.7 0.1 copy.17
  8.8 0.1 reshape.80
  8.9 38.7 %all-gather.2.cloned.1.call-done = bf16[1024,1024]{1,0:T(8,128)(2,1)} async-done(((bf16[128,1024]{1,0:T(8,128)(2,1)}), bf16[1024,1024]{1,0:T(8,128)(2,1)}) %all-gather.2.cloned.1.call-update) | async-done | bytes 2097168 | tf_op jit(solution)/shard_map/all_gather | solution.py:34
  47.6 0.0 copy-done
  47.6 2.9 %fusion.26 = f32[512,1024]{1,0:T(8,128)S(1)} fusion(bf16[1024,512]{1,0:T(8,128)(2,1)S(1)} %copy-done, bf16[1024,1024]{1,0:T(8,128)(2,1)} %all-gather.2.cloned.1.call-done), kind=kOutput, calls=%fused_computation.35 | convolution fusion | flops 1073741824 | bytes 5242880 | tf_op jit(solution)/shard_map/dot_general | solution.py:35
  50.4 2.6 %reshape.73 = f32[8,64,16,64]{3,2,1,0:T(8,128)} reshape(f32[512,1024]{1,0:T(8,128)S(1)} %fusion.26) | data formatting | bytes 4194304 | tf_op jit(solution)/shard_map/reshape | solution.py:38
  53.0 5.4 %copy.15 = f32[8,64,16,64]{3,1,2,0:T(8,128)} copy(f32[8,64,16,64]{3,2,1,0:T(8,128)} %reshape.73) | data formatting | bytes 4194304 | tf_op jit(solution)/shard_map/reshape | solution.py:38
  58.4 4.2 %gather_fusion = f32[64,64,64]{2,1,0:T(8,128)} fusion(f32[8,64,16,64]{3,1,2,0:T(8,128)} %copy.15, s32[64]{0:T(128)S(1)} %reshape.80), kind=kCustom, calls=%fused_computation | custom fusion | bytes 2097664 | tf_op jit(solution)/shard_map/jit(take_along_axis)/gather | solution.py:39
  62.6 1.8 %broadcast_select_fusion = f32[8,8,64,64]{3,2,1,0:T(8,128)S(1)} fusion(f32[8,8,64,64]{3,2,1,0:T(8,128)} %bitcast.57, pred[8,8]{1,0:T(8,128)(4,1)S(1)} %compare_and_fusion), kind=kLoop, calls=%fused_computation.8 | loop fusion | flops 262144 | bytes 2097216 | tf_op jit(solution)/shard_map/jit(take_along_axis)/select_n | solution.py:39
  64.4 2.3 %reshape.91 = f32[64,1,4096]{2,1,0:T(1,128)} reshape(f32[8,8,64,64]{3,2,1,0:T(8,128)S(1)} %broadcast_select_fusion) | data formatting | bytes 2097152 | tf_op jit(solution)/shard_map/reshape | solution.py:42
  66.7 0.0 copy-start.5
  66.7 71.4 %all_to_all.5 = f32[64,1,4096]{2,1,0:T(1,128)S(1)} all-to-all(f32[64,1,4096]{2,1,0:T(1,128)} %reshape.91), channel_id=1, replica_groups=mesh['dp'=64,'seq'=8] {'dp'}, dimensions={0} | all-to-all | bytes 2097152 | tf_op jit(solution)/shard_map/all_to_all | solution.py:43
  138.1 0.9 reduce_sum.9
  139.0 0.1 reshape.76
  139.1 0.8 fusion.2
  139.9 0.9 fusion.3
  140.7 0.2 fusion.17
  141.0 0.2 fusion.14
  141.2 0.3 fusion.10
  141.5 0.9 convolution_bitcast_fusion
  (11 shorter events, 0.0 us)
Async XLA Ops:
  7.2 40.4 %copy-start = (bf16[1024,512]{1,0:T(8,128)(2,1)S(1)}, bf16[1024,512]{1,0:T(8,128)(2,1)}, u32[]{:S(2)}) copy-start(bf16[1024,512]{1,0:T(8,128)(2,1)} %param.8) | copy-start | bytes 3145732
  7.2 40.4 %all-gather.2.cloned.1.call-start = ((), (), s32[]{:S(2)}) async-start(), calls=%async_computation.1 | async-start | bytes 2359296 | tf_op jit(solution)/shard_map/all_gather | solution.py:34
  66.6 72.4 %copy-start.3 = (f32[1,1,1,64,64]{4,3,2,1,0:T(8,128)S(1)}, f32[1,1,1,64,64]{4,3,2,1,0:T(8,128)}, u32[]{:S(2)}) copy-start(f32[1,1,1,64,64]{4,3,2,1,0:T(8,128)} %param.11) | copy-start | bytes 49156
  66.7 73.2 %copy-start.4 = (f32[1,1,1,64,64]{4,3,2,1,0:T(8,128)S(1)}, f32[1,1,1,64,64]{4,3,2,1,0:T(8,128)}, u32[]{:S(2)}) copy-start(f32[1,1,1,64,64]{4,3,2,1,0:T(8,128)} %param.12) | copy-start | bytes 49156
  66.7 74.1 %copy-start.2 = (f32[1,1,1,64,64]{4,3,2,1,0:T(8,128)S(1)}, f32[1,1,1,64,64]{4,3,2,1,0:T(8,128)}, u32[]{:S(2)}) copy-start(f32[1,1,1,64,64]{4,3,2,1,0:T(8,128)} %param.13) | copy-start | bytes 49156
  66.7 74.3 %copy-start.1 = (f32[1,1,1,64,64]{4,3,2,1,0:T(8,128)S(1)}, f32[1,1,1,64,64]{4,3,2,1,0:T(8,128)}, u32[]{:S(2)}) copy-start(f32[1,1,1,64,64]{4,3,2,1,0:T(8,128)} %param.14) | copy-start | bytes 49156
  66.7 74.6 %copy-start.5 = (f32[1,1,1,64,64]{4,3,2,1,0:T(8,128)S(1)}, f32[1,1,1,64,64]{4,3,2,1,0:T(8,128)}, u32[]{:S(2)}) copy-start(f32[1,1,1,64,64]{4,3,2,1,0:T(8,128)} %param.15) | copy-start | bytes 49156
Sparse Core Ops, SparseCore 0:
  10.1 37.3 all-gather.1
where the time goes:
time: 150 us; the launch traced here: 149 us
  blocking collectives  71.4 us (48%)
  waiting for transfers between devices  39.4 us (26%)
  local copies, waits for them, and re-layouts  15.4 us (10%)
  between operations  14.1 us (9%)
  matrix products  6.08 us (4%)
  other arithmetic  2.68 us (2%)
    all_to_all x1, blocking collectives, per_device(): lax.all_to_all(outgoing, 'dp', split_axis=0, concat_axis=0, tiled=True)  71.4 us
    all_gather x1, waiting for transfers between devices, per_device(): gathered = lax.all_gather(upstream, 'seq', axis=0, tiled=True)  38.7 us
    reshape x2, local copies, waits for them, and re-layouts, per_device(): tiles = grad.reshape(share_blocks, BLOCK, grad.shape[1] // BLOCK, BLOCK)  7.94 us
    gather x2, local copies, waits for them, and re-layouts, per_device(): picked = jnp.take_along_axis(tiles, kept_share[:, None, :, None], axis=2)  4.28 us
  transfers between devices with their start and end apart: 1, of which 1 were waited for; matrix products, arithmetic and copies ran while one was open for 1% of the time, Pallas kernels for 0%

commit v1 on v0

v1 whole, which is shorter than its diff:
```python
import jax
import jax.numpy as jnp
from jax import lax
from jax.experimental import pallas as pl
from jax.experimental.pallas import tpu as pltpu
from jax.sharding import Mesh, PartitionSpec as P

BLOCK = 64
HALF = BLOCK // 2
LANES = 128
DATA = ("zh", "zl", "x")
SEQ = ("y", "c")
HIGHEST = lax.Precision.HIGHEST


def grad_kernel(keep_ref, acts_ref, own_ref, other_ref, out_ref, tiles_ref):
    core = lax.axis_index("c")
    seq = lax.axis_index("y") * lax.axis_size("c") + core
    rows = acts_ref.shape[2] * acts_ref.shape[0]
    feats = acts_ref.shape[3]
    share_blocks = feats // BLOCK
    acts_own = acts_ref[:, core].reshape(rows, feats)
    acts_other = acts_ref[:, 1 - core].reshape(rows, feats)
    dims = (((0,), (0,)), ((), ()))
    for n in range(own_ref.shape[1] // 256):
        cols = slice(n * 256, n * 256 + 256)
        part = lax.dot_general(acts_own, own_ref[:, cols], dims, preferred_element_type=jnp.float32)
        part += lax.dot_general(
            acts_other, other_ref[:, cols], dims, preferred_element_type=jnp.float32
        )
        tiles_ref[2 * n] = part[:, :LANES]
        tiles_ref[2 * n + 1] = part[:, LANES:]
    left = lax.broadcasted_iota(jnp.int32, (HALF, LANES), 1) < BLOCK
    for r in range(share_blocks):
        for k in range(keep_ref.shape[0]):
            col = keep_ref[k, seq * share_blocks + r]
            tile = col // 2
            odd = (col % 2) == 1
            top = tiles_ref[tile, r * BLOCK : r * BLOCK + HALF, :]
            low = tiles_ref[tile, r * BLOCK + HALF : (r + 1) * BLOCK, :]
            top_side = jnp.where(odd, pltpu.roll(top, BLOCK, 1), top)
            low_side = jnp.where(odd, low, pltpu.roll(low, BLOCK, 1))
            out_ref[k, r * HALF : (r + 1) * HALF, :] = jnp.where(left, top_side, low_side)


def kept_partials(keep, acts, own, other):
    kept = keep.shape[0]
    feats = acts.shape[-1]
    return pl.pallas_call(
        grad_kernel,
        out_shape=jax.ShapeDtypeStruct((kept, feats // 2, LANES), jnp.float32),
        in_specs=[pl.BlockSpec(memory_space=pltpu.SMEM)]
        + [pl.BlockSpec(memory_space=pltpu.VMEM)] * 3,
        out_specs=pl.BlockSpec(memory_space=pltpu.VMEM),
        scratch_shapes=[pltpu.VMEM((own.shape[1] // LANES, feats, LANES), jnp.float32)],
        name="kept_partials",
    )(keep, acts, own, other)


def dot(a, b, ca, cb):
    return lax.dot_general(
        a, b, (((ca,), (cb,)), ((), ())), precision=HIGHEST, preferred_element_type=jnp.float32
    )


def step_kernel(parts_ref, lg_ref, rg_ref, lb_ref, rb_ref, sm_ref, nl_ref, nr_ref, dir_ref):
    packed = jnp.sum(parts_ref[...], axis=0)
    g = jnp.concatenate([packed[:, :BLOCK], packed[:, BLOCK:]], axis=0)
    lb = lb_ref[...]
    rb = rb_ref[...]
    rotated = dot(dot(lb, g, 0, 0), rb, 1, 0)
    second = 0.95 * sm_ref[...] + 0.05 * rotated * rotated
    scaled = rotated / (jnp.sqrt(second) + 1e-08)
    dir_ref[...] = dot(dot(lb, scaled, 1, 0), rb, 1, 1)
    nl_ref[...] = 0.95 * lg_ref[...] + 0.05 * dot(g, g, 1, 1)
    nr_ref[...] = 0.95 * rg_ref[...] + 0.05 * dot(g, g, 0, 0)


def soap_step(parts, *state):
    block = jax.ShapeDtypeStruct((BLOCK, BLOCK), jnp.float32)
    return pl.pallas_call(
        step_kernel,
        out_shape=(block, block, block),
        in_specs=[pl.BlockSpec(memory_space=pltpu.VMEM)] * 6,
        out_specs=[pl.BlockSpec(memory_space=pltpu.VMEM)] * 3,
        name="soap_step",
    )(parts, *state)


def per_device(acts, upstream, keep_lists, *state):
    tokens, cols = upstream.shape
    ny = lax.axis_size("y")
    spread = jnp.broadcast_to(upstream[None], (ny, tokens, cols))
    own = lax.all_to_all(spread, "y", split_axis=0, concat_axis=0, tiled=True)
    own = own.reshape(ny * tokens, cols)
    other = lax.ppermute(own, "c", [(0, 1), (1, 0)])
    packed = kept_partials(
        keep_lists.T, acts.reshape(ny, 2, tokens, acts.shape[1]), own, other
    )
    near = lax.all_to_all(packed, ("zl", "x"), split_axis=0, concat_axis=0, tiled=True)
    summed = jnp.sum(near, axis=0).reshape(-1, HALF, LANES)
    parts = lax.all_to_all(summed, "zh", split_axis=0, concat_axis=0, tiled=True)
    shape = state[0].shape
    outs = soap_step(parts, *[s.reshape(BLOCK, BLOCK) for s in state])
    return tuple(o.reshape(shape) for o in outs)


def solution(mesh):
    fine = Mesh(mesh.devices.reshape(8, 2, 4, 4, 2), DATA + SEQ)
    state = P(SEQ, DATA, None, None, None)
    in_specs = (P(DATA, SEQ), P(DATA + SEQ, None), P()) + (state,) * 5
    return jax.shard_map(
        per_device, mesh=fine, in_specs=in_specs, out_specs=(state,) * 3, check_vma=False
    )
```

time: 150 us -> 83.6 us (0.56)
  waiting for transfers between devices: 39.4 us -> 2.63 us
  between operations: 14.1 us -> 0.65 us
  local copies, waits for them, and re-layouts: 15.4 us -> 2.09 us
  Pallas kernels: 0 us -> 7.29 us
  matrix products: 6.08 us -> 0 us
  blocking collectives: 71.4 us -> 68.6 us
  other arithmetic: 2.68 us -> 0.06 us
  starting transfers between devices: 0.04 us -> 1.91 us
    all_gather x1 -> x0, waiting for transfers between devices: 38.7 us -> none  [per_device(): gathered = lax.all_gather(upstream, 'seq', axis=0, tiled=True)]
    reshape x3 -> x0, local copies, waits for them, and re-layouts: 10.2 us -> none  [the longest x2 7.94 us: per_device(): tiles = grad.reshape(share_blocks, BLOCK, grad.shape[1] // BLOCK, BLOCK)]
    pallas_call x0 -> x2, Pallas kernels: none -> 7.29 us  [the longest x1 4.84 us: kept_partials(): pl.pallas_call(grad_kernel, out_shape=jax.ShapeDtypeStruct((kept, feats /...]
    dot_general x7 -> x0, matrix products: 6.08 us -> none  [the longest x1 2.85 us: per_device(): lax.dot_general(acts, gathered, (((0,), (0,)), ((), ())), preferred_eleme...]
    gather x2 -> x0, local copies, waits for them, and re-layouts: 4.28 us -> none  [per_device(): picked = jnp.take_along_axis(tiles, kept_share[:, None, :, None], axis=2)]
    all_to_all x1 -> x3, blocking collectives: 71.4 us -> 68.6 us  [the longest x1 29.6 us: per_device(): lax.all_to_all(summed, 'zh', split_axis=0, concat_axis=0, tiled=True)]
    ppermute x0 -> x1, waiting for transfers between devices: none -> 2.63 us  [per_device(): other = lax.ppermute(own, 'c', [(0, 1), (1, 0)])]
    ppermute x0 -> x1, starting transfers between devices: none -> 1.91 us  [per_device(): other = lax.ppermute(own, 'c', [(0, 1), (1, 0)])]
  transfers between devices with their start and end apart: 1 -> 1, of which waited for: 1 -> 1; matrix products, arithmetic and copies ran while one was open for 1% -> 0% of each run, Pallas kernels for 0% -> 0%
where the time goes in v1:
time: 83.6 us; the launch traced here: 83.2 us
  blocking collectives  68.6 us (82%)
  Pallas kernels  7.29 us (9%)
  waiting for transfers between devices  2.63 us (3%)
  local copies, waits for them, and re-layouts  2.09 us (2%)
  starting transfers between devices  1.91 us (2%)
    all_to_all x1, blocking collectives, per_device(): lax.all_to_all(summed, 'zh', split_axis=0, concat_axis=0, tiled=True)  29.6 us
    all_to_all x1, blocking collectives, per_device(): lax.all_to_all(packed, ('zl', 'x'), split_axis=0, concat_axis=0, tiled=True)  19.6 us
    all_to_all x1, blocking collectives, per_device(): own = lax.all_to_all(spread, 'y', split_axis=0, concat_axis=0, tiled=True)  19.4 us
    pallas_call x1, Pallas kernels, kept_partials(): pl.pallas_call(grad_kernel, out_shape=jax.ShapeDtypeStruct((kept, feats /...  4.84 us
    ppermute x1, waiting for transfers between devices, per_device(): other = lax.ppermute(own, 'c', [(0, 1), (1, 0)])  2.63 us
    pallas_call x1, Pallas kernels, soap_step(): pl.pallas_call(step_kernel, out_shape=(block, block, block), in_specs=[pl...  2.45 us
    ppermute x1, starting transfers between devices, per_device(): other = lax.ppermute(own, 'c', [(0, 1), (1, 0)])  1.91 us
  transfers between devices with their start and end apart: 1, of which 1 were waited for; matrix products, arithmetic and copies ran while one was open for 0% of the time, Pallas kernels for 0%

profile of v1, /device:TPU:6, one launch (start us, length us, event | category | flops | bytes accessed | tf_op | source)
XLA Modules:
  0.0 83.2 jit_solution(7096464249368580554)
XLA Ops:
  0.6 1.1 %broadcast_in_dim.2 = bf16[4,128,1024]{2,1,0:T(8,128)(2,1)S(1)} broadcast(bf16[128,1024]{1,0:T(8,128)(2,1)} %param.9), dimensions={1,2} | broadcast | bytes 1310720 | tf_op jit(solution)/shard_map/broadcast_in_dim | solution.py:93
  1.7 19.4 %all_to_all.15 = bf16[4,128,1024]{2,1,0:T(8,128)(2,1)S(1)} all-to-all(bf16[4,128,1024]{2,1,0:T(8,128)(2,1)S(1)} %broadcast_in_dim.2), channel_id=1, replica_groups=mesh['zh'=8,'zl'=2,'x'=4,'y'=4,'c'=2] {'y'}, dimensions={0} | all-to-all | bytes 2097152 | tf_op jit(solution)/shard_map/all_to_all | solution.py:94
  21.1 0.0 copy-start
  21.1 1.9 %collective-permute-start = (bf16[512,1024]{1,0:T(8,128)(2,1)S(1)}, bf16[512,1024]{1,0:T(8,128)(2,1)S(1)}, u32[]{:S(2)}, u32[]{:S(2)}) collective-permute-start(bf16[512,1024]{1,0:T(8,128)(2,1)S(1)} %bitcast.12), channel_id=1, source_target_pairs={{0,1},{1,0},{2,3},{3,2},{4,5},{5,4},{6,7},{7,6},{8,9},{9,8},{10,11... | collective-permute-start | bytes 3145736 | tf_op jit(solution)/shard_map/ppermute | solution.py:96
  23.0 2.6 %collective-permute-done.other_ref = bf16[512,1024]{1,0:T(8,128)(2,1)S(1)} collective-permute-done((bf16[512,1024]{1,0:T(8,128)(2,1)S(1)}, bf16[512,1024]{1,0:T(8,128)(2,1)S(1)}, u32[]{:S(2)}, u32[]{:S(2)}) %collective-permute-start) | collective-permute-done | bytes 1048608 | tf_op jit(solution)/shard_map/ppermute | solution.py:96
  25.6 0.0 copy-start.1
  25.6 0.0 copy-done
  25.6 1.0 %copy-done.1 = bf16[512,1024]{1,0:T(8,128)(2,1)} copy-done((bf16[512,1024]{1,0:T(8,128)(2,1)}, bf16[512,1024]{1,0:T(8,128)(2,1)S(1)}, u32[]{:S(2)}) %copy-start.1) | copy-done | bytes 1048600
  26.6 4.8 %kept_partials.1 = f32[8,256,128]{2,1,0:T(8,128)} custom-call(s32[8,64]{1,0:T(8,128)} %bitcast.21, bf16[4,2,128,512]{3,2,1,0:T(8,128)(2,1)} %bitcast.14, bf16[512,1024]{1,0:T(8,128)(2,1)} %bitcast.13, bf16[512,1024]{1,0:T(8,128)(2,1)} %copy-done.1), custom_call_target="tpu_custom_call" | custom-call | tf_op jit(solution)/shard_map/kept_partials/pallas_call | solution.py:49
  31.5 19.6 %all_to_all.16 = f32[8,256,128]{2,1,0:T(8,128)S(1)} all-to-all(f32[8,256,128]{2,1,0:T(8,128)} %kept_partials.1), channel_id=1, replica_groups=mesh['zh'=8,'zl'=2,'x'=4,'y'=4,'c'=2] {'zl','x'}, dimensions={0} | all-to-all | bytes 2097152 | tf_op jit(solution)/shard_map/all_to_all | solution.py:100
  51.1 0.1 reduce_sum.9
  51.2 29.6 %all_to_all.17.parts_ref = f32[8,32,128]{2,1,0:T(8,128)} all-to-all(f32[8,32,128]{2,1,0:T(8,128)S(1)} %bitcast.15), channel_id=1, replica_groups=mesh['zh'=8,'zl'=2,'x'=4,'y'=4,'c'=2] {'zh'}, dimensions={0} | all-to-all | bytes 262144 | tf_op jit(solution)/shard_map/all_to_all | solution.py:102
  80.7 2.5 %soap_step.1 = (f32[64,64]{1,0:T(8,128)}, f32[64,64]{1,0:T(8,128)}, f32[64,64]{1,0:T(8,128)}) custom-call(f32[8,32,128]{2,1,0:T(8,128)} %all_to_all.17.parts_ref, f32[64,64]{1,0:T(8,128)} %bitcast.16, f32[64,64]{1,0:T(8,128)} %bitcast.17, f32[64,64]{1,0:T(8,128)} %bitcast.18, f32[64,64]{1,0:T(8,128)} %bitcast.19, f32[64,64]{1,0:T(8,128)} %bitcast.20), custom_call_target="tpu_custom_call" | custom-call | tf_op jit(solution)/shard_map/soap_step/pallas_call | solution.py:81
Async XLA Ops:
  21.1 4.5 %copy-start = (bf16[4,128,1024]{2,1,0:T(8,128)(2,1)}, bf16[4,128,1024]{2,1,0:T(8,128)(2,1)S(1)}, u32[]{:S(2)}) copy-start(bf16[4,128,1024]{2,1,0:T(8,128)(2,1)S(1)} %all_to_all.15) | copy-start | bytes 3145732
  21.1 4.5 %collective-permute-start = (bf16[512,1024]{1,0:T(8,128)(2,1)S(1)}, bf16[512,1024]{1,0:T(8,128)(2,1)S(1)}, u32[]{:S(2)}, u32[]{:S(2)}) collective-permute-start(bf16[512,1024]{1,0:T(8,128)(2,1)S(1)} %bitcast.12), channel_id=1, source_target_pairs={{0,1},{1,0},{2,3},{3,2},{4,5},{5,4},{6,7},{7,6},{8,9},{9,8},{10,11... | collective-permute-start | bytes 3145736 | tf_op jit(solution)/shard_map/ppermute | solution.py:96
  25.6 1.0 %copy-start.1 = (bf16[512,1024]{1,0:T(8,128)(2,1)}, bf16[512,1024]{1,0:T(8,128)(2,1)S(1)}, u32[]{:S(2)}) copy-start(bf16[512,1024]{1,0:T(8,128)(2,1)S(1)} %collective-permute-done.other_ref) | copy-start | bytes 3145732

commit v2 on v1

v2 whole, which is shorter than its diff:
```python
import jax
import jax.numpy as jnp
from jax import lax
from jax.experimental import pallas as pl
from jax.experimental.pallas import tpu as pltpu
from jax.sharding import Mesh, PartitionSpec as P

BLOCK = 64
HALF = BLOCK // 2
LANES = 128
DATA = ("zh", "zl", "x")
SEQ = ("y", "c")
SCALE = 1024.0
HIGHEST = lax.Precision.HIGHEST


def pack_kernel(keep_ref, grad_ref, out_ref):
    seq = lax.axis_index("y") * lax.axis_size("c") + lax.axis_index("c")
    share_blocks = grad_ref.shape[0] // BLOCK
    left = lax.broadcasted_iota(jnp.int32, (HALF, LANES), 1) < BLOCK
    for r in range(share_blocks):
        for k in range(keep_ref.shape[0]):
            col = keep_ref[k, seq * share_blocks + r]
            lanes = pl.ds(pl.multiple_of((col // 2) * LANES, LANES), LANES)
            odd = (col % 2) == 1
            top = grad_ref[r * BLOCK : r * BLOCK + HALF, lanes]
            low = grad_ref[r * BLOCK + HALF : (r + 1) * BLOCK, lanes]
            top_side = jnp.where(odd, pltpu.roll(top, BLOCK, 1), top)
            low_side = jnp.where(odd, low, pltpu.roll(low, BLOCK, 1))
            out_ref[k, r * HALF : (r + 1) * HALF, :] = jnp.where(left, top_side, low_side)


def pin(x):
    return pltpu.with_memory_space_constraint(x, pltpu.VMEM)


def pack_kept(keep, grad):
    kept = keep.shape[0]
    return pl.pallas_call(
        pack_kernel,
        out_shape=pltpu.VMEM((kept, grad.shape[0] // 2, LANES), jnp.float32),
        in_specs=[
            pl.BlockSpec(memory_space=pltpu.SMEM),
            pl.BlockSpec(memory_space=pltpu.VMEM),
        ],
        out_specs=pl.BlockSpec(memory_space=pltpu.VMEM),
        name="pack_kept",
    )(keep, pin(grad))


def dot(a, b, ca, cb):
    return lax.dot_general(
        a, b, (((ca,), (cb,)), ((), ())), precision=HIGHEST, preferred_element_type=jnp.float32
    )


def step_kernel(parts_ref, lg_ref, rg_ref, lb_ref, rb_ref, sm_ref, nl_ref, nr_ref, dir_ref):
    packed = jnp.sum(parts_ref[...], axis=0) * (1.0 / SCALE)
    g = jnp.concatenate([packed[:, :BLOCK], packed[:, BLOCK:]], axis=0)
    lb = lb_ref[...]
    rb = rb_ref[...]
    rotated = dot(dot(lb, g, 0, 0), rb, 1, 0)
    second = 0.95 * sm_ref[...] + 0.05 * rotated * rotated
    scaled = rotated / (jnp.sqrt(second) + 1e-08)
    dir_ref[...] = dot(dot(lb, scaled, 1, 0), rb, 1, 1)
    nl_ref[...] = 0.95 * lg_ref[...] + 0.05 * dot(g, g, 1, 1)
    nr_ref[...] = 0.95 * rg_ref[...] + 0.05 * dot(g, g, 0, 0)


def soap_step(parts, *state):
    out = jax.ShapeDtypeStruct((BLOCK, BLOCK), jnp.float32)
    return pl.pallas_call(
        step_kernel,
        out_shape=(out, out, out),
        in_specs=[pl.BlockSpec(memory_space=pltpu.VMEM)] * 6,
        out_specs=[pl.BlockSpec(memory_space=pltpu.VMEM)] * 3,
        name="soap_step",
    )(pin(parts), *[pin(s) for s in state])


def exchange(x, axes):
    return lax.all_to_all(x, axes, split_axis=0, concat_axis=0, tiled=True)


def per_device(acts, upstream, keep_lists, *state):
    tokens, cols = upstream.shape
    ny = lax.axis_size("y")
    spread = jnp.broadcast_to(upstream[None], (ny, tokens, cols))
    own = exchange(spread, "y")
    own = own.reshape(ny * tokens, cols)
    other = lax.ppermute(own, "c", [(0, 1), (1, 0)])
    mine = lax.axis_index("c")
    feats = acts.shape[1]
    halves = acts.reshape(ny, 2, tokens, feats)

    def term(core, rows):
        half = lax.dynamic_index_in_dim(halves, core, 1, keepdims=False)
        return lax.dot_general(
            half.reshape(ny * tokens, feats),
            rows,
            (((0,), (0,)), ((), ())),
            preferred_element_type=jnp.float32,
        )

    grad = term(mine, own) + term(1 - mine, other)
    packed = pack_kept(keep_lists.T, grad)
    near = exchange((packed * SCALE).astype(jnp.float16), ("zl", "x"))
    summed = jnp.sum(near.astype(jnp.float32), axis=0).reshape(-1, HALF, LANES)
    parts = exchange(summed, "zh")
    shape = state[0].shape
    outs = soap_step(parts, *[s.reshape(BLOCK, BLOCK) for s in state])
    return tuple(o.reshape(shape) for o in outs)


def solution(mesh):
    fine = Mesh(mesh.devices.reshape(8, 2, 4, 4, 2), DATA + SEQ)
    state = P(SEQ, DATA, None, None, None)
    in_specs = (P(DATA, SEQ), P(DATA + SEQ, None), P()) + (state,) * 5
    return jax.shard_map(
        per_device, mesh=fine, in_specs=in_specs, out_specs=(state,) * 3, check_vma=False
    )
```

time: 83.6 us -> 73.3 us (0.88)
  blocking collectives: 68.6 us -> 62.7 us
  Pallas kernels: 7.29 us -> 2.86 us
  matrix products: 0 us -> 1.45 us
    all_to_all x3, blocking collectives: 68.6 us -> 62.7 us  [exchange(): return lax.all_to_all(x, axes, split_axis=0, concat_axis=0, tiled=True)]
    pallas_call x2, Pallas kernels: 7.29 us -> 2.86 us  [the longest x1 1.51 us: soap_step(): pl.pallas_call(step_kernel, out_shape=(out, out, out), in_specs=[pl.Block...]
    dot_general x0 -> x2, matrix products: none -> 1.45 us  [term(): lax.dot_general(half.reshape(ny * tokens, feats), rows, (((0,), (0,)), ((...]
    unnamed x4 -> x12, local copies, waits for them, and re-layouts: 1.03 us -> 0.04 us
  transfers between devices with their start and end apart: 1 -> 1, of which waited for: 1 -> 1; matrix products, arithmetic and copies ran while one was open for 0% -> 1% of each run, Pallas kernels for 0% -> 0%
where the time goes in v2:
time: 73.3 us; the launch traced here: 72.9 us
  blocking collectives  62.7 us (86%)
  Pallas kernels  2.86 us (4%)
  starting transfers between devices  1.91 us (3%)
  waiting for transfers between devices  1.8 us (2%)
  matrix products  1.45 us (2%)
  local copies, waits for them, and re-layouts  1.27 us (2%)
  between operations  0.76 us (1%)
    all_to_all x3, blocking collectives, exchange(): return lax.all_to_all(x, axes, split_axis=0, concat_axis=0, tiled=True)  62.7 us
    ppermute x1, starting transfers between devices, per_device(): other = lax.ppermute(own, 'c', [(0, 1), (1, 0)])  1.91 us
    ppermute x1, waiting for transfers between devices, per_device(): other = lax.ppermute(own, 'c', [(0, 1), (1, 0)])  1.8 us
    pallas_call x1, Pallas kernels, soap_step(): pl.pallas_call(step_kernel, out_shape=(out, out, out), in_specs=[pl.Block...  1.51 us
  transfers between devices with their start and end apart: 1, of which 1 were waited for; matrix products, arithmetic and copies ran while one was open for 1% of the time, Pallas kernels for 0%

profile of v2, /device:TPU:6, one launch (start us, length us, event | category | flops | bytes accessed | tf_op | source)
XLA Modules:
  0.0 72.9 jit_solution(16881828185619363040)
XLA Ops:
  0.6 0.0 copy-start.5
  0.6 1.2 %broadcast_in_dim.2 = bf16[4,128,1024]{2,1,0:T(8,128)(2,1)S(1)} broadcast(bf16[128,1024]{1,0:T(8,128)(2,1)} %param.9), dimensions={1,2} | broadcast | bytes 1310720 | tf_op jit(solution)/shard_map/broadcast_in_dim | solution.py:88
  1.8 19.4 %all_to_all.15 = bf16[4,128,1024]{2,1,0:T(8,128)(2,1)S(1)} all-to-all(bf16[4,128,1024]{2,1,0:T(8,128)(2,1)S(1)} %broadcast_in_dim.2), channel_id=1, replica_groups=mesh['zh'=8,'zl'=2,'x'=4,'y'=4,'c'=2] {'y'}, dimensions={0} | all-to-all | bytes 2097152 | tf_op jit(solution)/shard_map/all_to_all | solution.py:82
  21.2 1.9 %collective-permute-start = (bf16[512,1024]{1,0:T(8,128)(2,1)S(1)}, bf16[512,1024]{1,0:T(8,128)(2,1)S(1)}, u32[]{:S(2)}, u32[]{:S(2)}) collective-permute-start(bf16[512,1024]{1,0:T(8,128)(2,1)S(1)} %bitcast.23), channel_id=1, source_target_pairs={{0,1},{1,0},{2,3},{3,2},{4,5},{5,4},{6,7},{7,6},{8,9},{9,8},{10,11... | collective-permute-start | bytes 3145736 | tf_op jit(solution)/shard_map/ppermute | solution.py:91
  23.1 0.0 copy-done.5
  23.1 0.1 constant_dynamic-slice_fusion
  23.2 0.7 fusion
  23.9 1.8 %collective-permute-done = bf16[512,1024]{1,0:T(8,128)(2,1)S(1)} collective-permute-done((bf16[512,1024]{1,0:T(8,128)(2,1)S(1)}, bf16[512,1024]{1,0:T(8,128)(2,1)S(1)}, u32[]{:S(2)}, u32[]{:S(2)}) %collective-permute-start) | collective-permute-done | bytes 1048608 | tf_op jit(solution)/shard_map/ppermute | solution.py:91
  25.7 0.7 convolution_add_fusion.grad_ref
  26.4 1.4 %pack_kept.1 = f32[8,256,128]{2,1,0:T(8,128)S(1)} custom-call(s32[8,64]{1,0:T(8,128)} %bitcast.29, f32[512,1024]{1,0:T(8,128)S(1)} %convolution_add_fusion.grad_ref), custom_call_target="tpu_custom_call" | custom-call | tf_op jit(solution)/shard_map/pack_kept/pallas_call | solution.py:39
  27.8 0.0 copy-start
  27.8 0.0 copy-start.1
  27.8 0.0 copy-start.2
  27.8 0.0 copy-start.3
  27.8 0.0 copy-start.4
  27.9 0.1 multiply_convert_fusion
  28.0 13.8 %all_to_all.16 = f16[8,256,128]{2,1,0:T(8,128)(2,1)S(1)} all-to-all(f16[8,256,128]{2,1,0:T(8,128)(2,1)S(1)} %multiply_convert_fusion), channel_id=1, replica_groups=mesh['zh'=8,'zl'=2,'x'=4,'y'=4,'c'=2] {'zl','x'}, dimensions={0} | all-to-all | bytes 1048576 | tf_op jit(solution)/shard_map/all_to_all | solution.py:82
  41.8 0.1 convert_reduce_fusion
  41.9 29.5 %all_to_all.17.parts_ref = f32[8,32,128]{2,1,0:T(8,128)S(1)} all-to-all(f32[8,32,128]{2,1,0:T(8,128)S(1)} %bitcast.28), channel_id=1, replica_groups=mesh['zh'=8,'zl'=2,'x'=4,'y'=4,'c'=2] {'zh'}, dimensions={0} | all-to-all | bytes 262144 | tf_op jit(solution)/shard_map/all_to_all | solution.py:82
  71.3 0.0 copy-done
  71.3 0.0 copy-done.1
  71.3 0.0 copy-done.2
  71.3 0.0 copy-done.3
  71.4 1.5 %soap_step.1 = (f32[64,64]{1,0:T(8,128)}, f32[64,64]{1,0:T(8,128)}, f32[64,64]{1,0:T(8,128)}) custom-call(f32[8,32,128]{2,1,0:T(8,128)S(1)} %all_to_all.17.parts_ref, f32[64,64]{1,0:T(8,128)S(1)} %bitcast.18, f32[64,64]{1,0:T(8,128)S(1)} %bitcast.19, f32[64,64]{1,0:T(8,128)S(1)} %bitcast.20, f32[64,64]{1,0:T(8,128)S(1)} %bitcast.21, f32[64,64]{1,0:T(8,128)S(1)} %bitcast.22), custom_call_target="tpu_custom_call" | custom-call | tf_op jit(solution)/shard_map/soap_step/pallas_call | solution.py:72
  (1 shorter events, 0.0 us)
Async XLA Ops:
  0.6 22.5 %copy-start.5 = (bf16[1024,512]{1,0:T(8,128)(2,1)S(1)}, bf16[1024,512]{1,0:T(8,128)(2,1)}, u32[]{:S(2)}) copy-start(bf16[1024,512]{1,0:T(8,128)(2,1)} %param.8) | copy-start | bytes 3145732
  21.2 4.5 %collective-permute-start = (bf16[512,1024]{1,0:T(8,128)(2,1)S(1)}, bf16[512,1024]{1,0:T(8,128)(2,1)S(1)}, u32[]{:S(2)}, u32[]{:S(2)}) collective-permute-start(bf16[512,1024]{1,0:T(8,128)(2,1)S(1)} %bitcast.23), channel_id=1, source_target_pairs={{0,1},{1,0},{2,3},{3,2},{4,5},{5,4},{6,7},{7,6},{8,9},{9,8},{10,11... | collective-permute-start | bytes 3145736 | tf_op jit(solution)/shard_map/ppermute | solution.py:91
  27.8 43.5 %copy-start = (f32[1,1,1,64,64]{4,3,2,1,0:T(8,128)S(1)}, f32[1,1,1,64,64]{4,3,2,1,0:T(8,128)}, u32[]{:S(2)}) copy-start(f32[1,1,1,64,64]{4,3,2,1,0:T(8,128)} %param.11) | copy-start | bytes 49156
  27.8 43.5 %copy-start.1 = (f32[1,1,1,64,64]{4,3,2,1,0:T(8,128)S(1)}, f32[1,1,1,64,64]{4,3,2,1,0:T(8,128)}, u32[]{:S(2)}) copy-start(f32[1,1,1,64,64]{4,3,2,1,0:T(8,128)} %param.12) | copy-start | bytes 49156
  27.8 43.5 %copy-start.2 = (f32[1,1,1,64,64]{4,3,2,1,0:T(8,128)S(1)}, f32[1,1,1,64,64]{4,3,2,1,0:T(8,128)}, u32[]{:S(2)}) copy-start(f32[1,1,1,64,64]{4,3,2,1,0:T(8,128)} %param.13) | copy-start | bytes 49156
  27.8 43.5 %copy-start.3 = (f32[1,1,1,64,64]{4,3,2,1,0:T(8,128)S(1)}, f32[1,1,1,64,64]{4,3,2,1,0:T(8,128)}, u32[]{:S(2)}) copy-start(f32[1,1,1,64,64]{4,3,2,1,0:T(8,128)} %param.14) | copy-start | bytes 49156
  27.8 43.5 %copy-start.4 = (f32[1,1,1,64,64]{4,3,2,1,0:T(8,128)S(1)}, f32[1,1,1,64,64]{4,3,2,1,0:T(8,128)}, u32[]{:S(2)}) copy-start(f32[1,1,1,64,64]{4,3,2,1,0:T(8,128)} %param.15) | copy-start | bytes 49156

commit v3 on v2

--- a/solution.py
+++ b/solution.py
@@ -11,16 +11,20 @@
 DATA = ("zh", "zl", "x")
 SEQ = ("y", "c")
 SCALE = 1024.0
-HIGHEST = lax.Precision.HIGHEST
+PRECISION = lax.Precision.HIGH
 
 
 def pack_kernel(keep_ref, grad_ref, out_ref):
     seq = lax.axis_index("y") * lax.axis_size("c") + lax.axis_index("c")
     share_blocks = grad_ref.shape[0] // BLOCK
     left = lax.broadcasted_iota(jnp.int32, (HALF, LANES), 1) < BLOCK
-    for r in range(share_blocks):
+    keep = keep_ref[...]
+    coded = keep << (4 * lax.broadcasted_iota(jnp.int32, keep.shape, 0))
+    block = lax.broadcasted_iota(jnp.int32, keep.shape, 1) - seq * share_blocks
+    codes = [jnp.sum(jnp.where(block == r, coded, 0)) for r in range(share_blocks)]
+    for r, code in enumerate(codes):
         for k in range(keep_ref.shape[0]):
-            col = keep_ref[k, seq * share_blocks + r]
+            col = (code >> (4 * k)) & 15
             lanes = pl.ds(pl.multiple_of((col // 2) * LANES, LANES), LANES)
             odd = (col % 2) == 1
             top = grad_ref[r * BLOCK : r * BLOCK + HALF, lanes]
@@ -39,18 +43,15 @@
     return pl.pallas_call(
         pack_kernel,
         out_shape=pltpu.VMEM((kept, grad.shape[0] // 2, LANES), jnp.float32),
-        in_specs=[
-            pl.BlockSpec(memory_space=pltpu.SMEM),
-            pl.BlockSpec(memory_space=pltpu.VMEM),
-        ],
+        in_specs=[pl.BlockSpec(memory_space=pltpu.VMEM)] * 2,
         out_specs=pl.BlockSpec(memory_space=pltpu.VMEM),
         name="pack_kept",
-    )(keep, pin(grad))
+    )(pin(keep), pin(grad))
 
 
 def dot(a, b, ca, cb):
     return lax.dot_general(
-        a, b, (((ca,), (cb,)), ((), ())), precision=HIGHEST, preferred_element_type=jnp.float32
+        a, b, (((ca,), (cb,)), ((), ())), precision=PRECISION, preferred_element_type=jnp.float32
     )
 
 

time: 73.3 us -> 72.6 us (level)
  no operation moved by 1% of the time
where the time goes in v3:
time: 72.6 us; the launch traced here: 72.2 us
  blocking collectives  62.7 us (86%)
  Pallas kernels  2.14 us (3%)
  starting transfers between devices  1.91 us (3%)
  waiting for transfers between devices  1.8 us (2%)
  matrix products  1.47 us (2%)
  local copies, waits for them, and re-layouts  1.27 us (2%)
  between operations  0.77 us (1%)
    all_to_all x3, blocking collectives, exchange(): return lax.all_to_all(x, axes, split_axis=0, concat_axis=0, tiled=True)  62.7 us
    ppermute x1, starting transfers between devices, per_device(): other = lax.ppermute(own, 'c', [(0, 1), (1, 0)])  1.91 us
    ppermute x1, waiting for transfers between devices, per_device(): other = lax.ppermute(own, 'c', [(0, 1), (1, 0)])  1.8 us
    dot_general x2, matrix products, term(): lax.dot_general(half.reshape(ny * tokens, feats), rows, (((0,), (0,)), ((...  1.47 us
  transfers between devices with their start and end apart: 1, of which 1 were waited for; matrix products, arithmetic and copies ran while one was open for 1% of the time, Pallas kernels for 0%

profile of v3, /device:TPU:6, one launch (start us, length us, event | category | flops | bytes accessed | tf_op | source)
XLA Modules:
  0.0 72.2 jit_solution(9668220128750272975)
XLA Ops:
  0.6 0.0 copy-start.6
  0.6 1.2 %broadcast_in_dim.2 = bf16[4,128,1024]{2,1,0:T(8,128)(2,1)S(1)} broadcast(bf16[128,1024]{1,0:T(8,128)(2,1)} %param.9), dimensions={1,2} | broadcast | bytes 1310720 | tf_op jit(solution)/shard_map/broadcast_in_dim | solution.py:89
  1.8 19.4 %all_to_all.15 = bf16[4,128,1024]{2,1,0:T(8,128)(2,1)S(1)} all-to-all(bf16[4,128,1024]{2,1,0:T(8,128)(2,1)S(1)} %broadcast_in_dim.2), channel_id=1, replica_groups=mesh['zh'=8,'zl'=2,'x'=4,'y'=4,'c'=2] {'y'}, dimensions={0} | all-to-all | bytes 2097152 | tf_op jit(solution)/shard_map/all_to_all | solution.py:83
  21.2 1.9 %collective-permute-start = (bf16[512,1024]{1,0:T(8,128)(2,1)S(1)}, bf16[512,1024]{1,0:T(8,128)(2,1)S(1)}, u32[]{:S(2)}, u32[]{:S(2)}) collective-permute-start(bf16[512,1024]{1,0:T(8,128)(2,1)S(1)} %bitcast.24), channel_id=1, source_target_pairs={{0,1},{1,0},{2,3},{3,2},{4,5},{5,4},{6,7},{7,6},{8,9},{9,8},{10,11... | collective-permute-start | bytes 3145736 | tf_op jit(solution)/shard_map/ppermute | solution.py:92
  23.1 0.0 copy-done.6
  23.1 0.1 constant_dynamic-slice_fusion
  23.2 0.7 %fusion = f32[512,1024]{1,0:T(8,128)S(1)} fusion(bf16[512,512]{1,0:T(8,128)(2,1)S(1)} %bitcast.26, bf16[512,1024]{1,0:T(8,128)(2,1)S(1)} %bitcast.25), kind=kOutput, calls=%fused_computation.5 | convolution fusion | flops 536870912 | bytes 3670016 | tf_op jit(solution)/shard_map/dot_general | solution.py:99
  23.9 1.8 %collective-permute-done = bf16[512,1024]{1,0:T(8,128)(2,1)S(1)} collective-permute-done((bf16[512,1024]{1,0:T(8,128)(2,1)S(1)}, bf16[512,1024]{1,0:T(8,128)(2,1)S(1)}, u32[]{:S(2)}, u32[]{:S(2)}) %collective-permute-start) | collective-permute-done | bytes 1048608 | tf_op jit(solution)/shard_map/ppermute | solution.py:92
  25.7 0.7 %convolution_add_fusion.grad_ref = f32[512,1024]{1,0:T(8,128)S(1)} fusion(f32[512,1024]{1,0:T(8,128)S(1)} %fusion, bf16[512,512]{1,0:T(8,128)(2,1)S(1)} %bitcast.27, bf16[512,1024]{1,0:T(8,128)(2,1)S(1)} %collective-permute-done), kind=kOutput, calls=%fused_computation | convolution fusion | flops 537395200 | bytes 5767168 | tf_op jit(solution)/shard_map/dot_general | solution.py:99
  26.5 0.0 copy-done.5
  26.5 0.8 %pack_kept.1 = f32[8,256,128]{2,1,0:T(8,128)S(1)} custom-call(s32[8,64]{1,0:T(8,128)S(1)} %bitcast.23, f32[512,1024]{1,0:T(8,128)S(1)} %convolution_add_fusion.grad_ref), custom_call_target="tpu_custom_call" | custom-call | tf_op jit(solution)/shard_map/pack_kept/pallas_call | solution.py:43
  27.3 0.0 copy-start
  27.3 0.0 copy-start.1
  27.3 0.0 copy-start.2
  27.3 0.0 copy-start.3
  27.3 0.0 copy-start.4
  27.3 0.1 multiply_convert_fusion
  27.5 13.8 %all_to_all.16 = f16[8,256,128]{2,1,0:T(8,128)(2,1)S(1)} all-to-all(f16[8,256,128]{2,1,0:T(8,128)(2,1)S(1)} %multiply_convert_fusion), channel_id=1, replica_groups=mesh['zh'=8,'zl'=2,'x'=4,'y'=4,'c'=2] {'zl','x'}, dimensions={0} | all-to-all | bytes 1048576 | tf_op jit(solution)/shard_map/all_to_all | solution.py:83
  41.3 0.1 convert_reduce_fusion
  41.4 29.5 %all_to_all.17.parts_ref = f32[8,32,128]{2,1,0:T(8,128)S(1)} all-to-all(f32[8,32,128]{2,1,0:T(8,128)S(1)} %bitcast.29), channel_id=1, replica_groups=mesh['zh'=8,'zl'=2,'x'=4,'y'=4,'c'=2] {'zh'}, dimensions={0} | all-to-all | bytes 262144 | tf_op jit(solution)/shard_map/all_to_all | solution.py:83
  70.8 0.0 copy-done
  70.8 0.0 copy-done.1
  70.8 0.0 copy-done.2
  70.9 1.3 %soap_step.1 = (f32[64,64]{1,0:T(8,128)}, f32[64,64]{1,0:T(8,128)}, f32[64,64]{1,0:T(8,128)}) custom-call(f32[8,32,128]{2,1,0:T(8,128)S(1)} %all_to_all.17.parts_ref, f32[64,64]{1,0:T(8,128)S(1)} %bitcast.18, f32[64,64]{1,0:T(8,128)S(1)} %bitcast.19, f32[64,64]{1,0:T(8,128)S(1)} %bitcast.20, f32[64,64]{1,0:T(8,128)S(1)} %bitcast.21, f32[64,64]{1,0:T(8,128)S(1)} %bitcast.22), custom_call_target="tpu_custom_call" | custom-call | tf_op jit(solution)/shard_map/soap_step/pallas_call | solution.py:73
  (3 shorter events, 0.0 us)
Async XLA Ops:
  0.6 22.5 %copy-start.6 = (bf16[1024,512]{1,0:T(8,128)(2,1)S(1)}, bf16[1024,512]{1,0:T(8,128)(2,1)}, u32[]{:S(2)}) copy-start(bf16[1024,512]{1,0:T(8,128)(2,1)} %param.8) | copy-start | bytes 3145732
  21.2 4.5 %collective-permute-start = (bf16[512,1024]{1,0:T(8,128)(2,1)S(1)}, bf16[512,1024]{1,0:T(8,128)(2,1)S(1)}, u32[]{:S(2)}, u32[]{:S(2)}) collective-permute-start(bf16[512,1024]{1,0:T(8,128)(2,1)S(1)} %bitcast.24), channel_id=1, source_target_pairs={{0,1},{1,0},{2,3},{3,2},{4,5},{5,4},{6,7},{7,6},{8,9},{9,8},{10,11... | collective-permute-start | bytes 3145736 | tf_op jit(solution)/shard_map/ppermute | solution.py:92
  25.7 0.8 %copy-start.5 = (s32[64,8]{0,1:T(8,128)S(1)}, s32[64,8]{0,1:T(8,128)}, u32[]{:S(2)}) copy-start(s32[64,8]{0,1:T(8,128)} %param.10) | copy-start | bytes 6148
  27.3 43.5 %copy-start = (f32[1,1,1,64,64]{4,3,2,1,0:T(8,128)S(1)}, f32[1,1,1,64,64]{4,3,2,1,0:T(8,128)}, u32[]{:S(2)}) copy-start(f32[1,1,1,64,64]{4,3,2,1,0:T(8,128)} %param.11) | copy-start | bytes 49156
  27.3 43.5 %copy-start.1 = (f32[1,1,1,64,64]{4,3,2,1,0:T(8,128)S(1)}, f32[1,1,1,64,64]{4,3,2,1,0:T(8,128)}, u32[]{:S(2)}) copy-start(f32[1,1,1,64,64]{4,3,2,1,0:T(8,128)} %param.12) | copy-start | bytes 49156
  27.3 43.5 %copy-start.2 = (f32[1,1,1,64,64]{4,3,2,1,0:T(8,128)S(1)}, f32[1,1,1,64,64]{4,3,2,1,0:T(8,128)}, u32[]{:S(2)}) copy-start(f32[1,1,1,64,64]{4,3,2,1,0:T(8,128)} %param.13) | copy-start | bytes 49156
  27.3 43.5 %copy-start.3 = (f32[1,1,1,64,64]{4,3,2,1,0:T(8,128)S(1)}, f32[1,1,1,64,64]{4,3,2,1,0:T(8,128)}, u32[]{:S(2)}) copy-start(f32[1,1,1,64,64]{4,3,2,1,0:T(8,128)} %param.14) | copy-start | bytes 49156
  27.3 43.5 %copy-start.4 = (f32[1,1,1,64,64]{4,3,2,1,0:T(8,128)S(1)}, f32[1,1,1,64,64]{4,3,2,1,0:T(8,128)}, u32[]{:S(2)}) copy-start(f32[1,1,1,64,64]{4,3,2,1,0:T(8,128)} %param.15) | copy-start | bytes 49156

commit v4 on v3

--- a/solution.py
+++ b/solution.py
@@ -11,6 +11,7 @@
 DATA = ("zh", "zl", "x")
 SEQ = ("y", "c")
 SCALE = 1024.0
+FAR_ORDER = (0, 4, 2, 6, 1, 5, 3, 7)
 PRECISION = lax.Precision.HIGH
 
 
@@ -31,7 +32,8 @@
             low = grad_ref[r * BLOCK + HALF : (r + 1) * BLOCK, lanes]
             top_side = jnp.where(odd, pltpu.roll(top, BLOCK, 1), top)
             low_side = jnp.where(odd, low, pltpu.roll(low, BLOCK, 1))
-            out_ref[k, r * HALF : (r + 1) * HALF, :] = jnp.where(left, top_side, low_side)
+            spot = FAR_ORDER.index(r) * HALF
+            out_ref[k, spot : spot + HALF, :] = jnp.where(left, top_side, low_side)
 
 
 def pin(x):
@@ -79,8 +81,11 @@
     )(pin(parts), *[pin(s) for s in state])
 
 
-def exchange(x, axes):
-    return lax.all_to_all(x, axes, split_axis=0, concat_axis=0, tiled=True)
+def exchange(x, axes, order=None):
+    groups = None if order is None else [list(order)]
+    return lax.all_to_all(
+        x, axes, split_axis=0, concat_axis=0, tiled=True, axis_index_groups=groups
+    )
 
 
 def per_device(acts, upstream, keep_lists, *state):
@@ -107,7 +112,7 @@
     packed = pack_kept(keep_lists.T, grad)
     near = exchange((packed * SCALE).astype(jnp.float16), ("zl", "x"))
     summed = jnp.sum(near.astype(jnp.float32), axis=0).reshape(-1, HALF, LANES)
-    parts = exchange(summed, "zh")
+    parts = exchange(summed, "zh", FAR_ORDER)
     shape = state[0].shape
     outs = soap_step(parts, *[s.reshape(BLOCK, BLOCK) for s in state])
     return tuple(o.reshape(shape) for o in outs)

time: 72.6 us -> 70.9 us (0.977)
  blocking collectives: 62.7 us -> 60.4 us
    all_to_all x3, blocking collectives: 62.7 us -> 60.4 us  [exchange(): lax.all_to_all(x, axes, split_axis=0, concat_axis=0, tiled=True, axis_ind...]
where the time goes in v4:
time: 70.9 us; the launch traced here: 70 us
  blocking collectives  60.4 us (85%)
  Pallas kernels  2.14 us (3%)
  starting transfers between devices  1.91 us (3%)
  waiting for transfers between devices  1.8 us (3%)
  matrix products  1.47 us (2%)
  local copies, waits for them, and re-layouts  1.27 us (2%)
  between operations  0.77 us (1%)
    all_to_all x3, blocking collectives, exchange(): lax.all_to_all(x, axes, split_axis=0, concat_axis=0, tiled=True, axis_ind...  60.4 us
    ppermute x1, starting transfers between devices, per_device(): other = lax.ppermute(own, 'c', [(0, 1), (1, 0)])  1.91 us
    ppermute x1, waiting for transfers between devices, per_device(): other = lax.ppermute(own, 'c', [(0, 1), (1, 0)])  1.8 us
    dot_general x2, matrix products, term(): lax.dot_general(half.reshape(ny * tokens, feats), rows, (((0,), (0,)), ((...  1.47 us
  transfers between devices with their start and end apart: 1, of which 1 were waited for; matrix products, arithmetic and copies ran while one was open for 1% of the time, Pallas kernels for 0%

profile of v4, /device:TPU:6, one launch (start us, length us, event | category | flops | bytes accessed | tf_op | source)
XLA Modules:
  0.0 70.0 jit_solution(11235663746450199836)
XLA Ops:
  0.6 0.0 copy-start.6
  0.6 1.2 %broadcast_in_dim.2 = bf16[4,128,1024]{2,1,0:T(8,128)(2,1)S(1)} broadcast(bf16[128,1024]{1,0:T(8,128)(2,1)} %param.9), dimensions={1,2} | broadcast | bytes 1310720 | tf_op jit(solution)/shard_map/broadcast_in_dim | solution.py:94
  1.8 19.4 %all_to_all.15 = bf16[4,128,1024]{2,1,0:T(8,128)(2,1)S(1)} all-to-all(bf16[4,128,1024]{2,1,0:T(8,128)(2,1)S(1)} %broadcast_in_dim.2), channel_id=1, replica_groups=mesh['zh'=8,'zl'=2,'x'=4,'y'=4,'c'=2] {'y'}, dimensions={0} | all-to-all | bytes 2097152 | tf_op jit(solution)/shard_map/all_to_all | solution.py:86
  21.2 1.9 %collective-permute-start = (bf16[512,1024]{1,0:T(8,128)(2,1)S(1)}, bf16[512,1024]{1,0:T(8,128)(2,1)S(1)}, u32[]{:S(2)}, u32[]{:S(2)}) collective-permute-start(bf16[512,1024]{1,0:T(8,128)(2,1)S(1)} %bitcast.24), channel_id=1, source_target_pairs={{0,1},{1,0},{2,3},{3,2},{4,5},{5,4},{6,7},{7,6},{8,9},{9,8},{10,11... | collective-permute-start | bytes 3145736 | tf_op jit(solution)/shard_map/ppermute | solution.py:97
  23.1 0.0 copy-done.6
  23.1 0.1 constant_dynamic-slice_fusion
  23.2 0.7 %fusion = f32[512,1024]{1,0:T(8,128)S(1)} fusion(bf16[512,512]{1,0:T(8,128)(2,1)S(1)} %bitcast.26, bf16[512,1024]{1,0:T(8,128)(2,1)S(1)} %bitcast.25), kind=kOutput, calls=%fused_computation.5 | convolution fusion | flops 536870912 | bytes 3670016 | tf_op jit(solution)/shard_map/dot_general | solution.py:104
  23.9 1.8 %collective-permute-done = bf16[512,1024]{1,0:T(8,128)(2,1)S(1)} collective-permute-done((bf16[512,1024]{1,0:T(8,128)(2,1)S(1)}, bf16[512,1024]{1,0:T(8,128)(2,1)S(1)}, u32[]{:S(2)}, u32[]{:S(2)}) %collective-permute-start) | collective-permute-done | bytes 1048608 | tf_op jit(solution)/shard_map/ppermute | solution.py:97
  25.7 0.7 %convolution_add_fusion.grad_ref = f32[512,1024]{1,0:T(8,128)S(1)} fusion(f32[512,1024]{1,0:T(8,128)S(1)} %fusion, bf16[512,512]{1,0:T(8,128)(2,1)S(1)} %bitcast.27, bf16[512,1024]{1,0:T(8,128)(2,1)S(1)} %collective-permute-done), kind=kOutput, calls=%fused_computation | convolution fusion | flops 537395200 | bytes 5767168 | tf_op jit(solution)/shard_map/dot_general | solution.py:104
  26.5 0.0 copy-done.5
  26.5 0.8 %pack_kept.1 = f32[8,256,128]{2,1,0:T(8,128)S(1)} custom-call(s32[8,64]{1,0:T(8,128)S(1)} %bitcast.23, f32[512,1024]{1,0:T(8,128)S(1)} %convolution_add_fusion.grad_ref), custom_call_target="tpu_custom_call" | custom-call | tf_op jit(solution)/shard_map/pack_kept/pallas_call | solution.py:45
  27.3 0.0 copy-start
  27.3 0.0 copy-start.1
  27.3 0.0 copy-start.2
  27.3 0.0 copy-start.3
  27.3 0.0 copy-start.4
  27.3 0.1 multiply_convert_fusion
  27.5 13.8 %all_to_all.16 = f16[8,256,128]{2,1,0:T(8,128)(2,1)S(1)} all-to-all(f16[8,256,128]{2,1,0:T(8,128)(2,1)S(1)} %multiply_convert_fusion), channel_id=1, replica_groups=mesh['zh'=8,'zl'=2,'x'=4,'y'=4,'c'=2] {'zl','x'}, dimensions={0} | all-to-all | bytes 1048576 | tf_op jit(solution)/shard_map/all_to_all | solution.py:86
  41.3 0.1 convert_reduce_fusion
  41.4 27.2 %all_to_all.17.parts_ref = f32[8,32,128]{2,1,0:T(8,128)S(1)} all-to-all(f32[8,32,128]{2,1,0:T(8,128)S(1)} %bitcast.29), channel_id=1, replica_groups={{0,256,128,384,64,320,192,448},{1,257,129,385,65,321,193,449},{2,258,13..., dimensions={0} | all-to-all | bytes 262144 | tf_op jit(solution)/shard_map/all_to_all | solution.py:86
  68.6 0.0 copy-done
  68.6 0.0 copy-done.1
  68.6 0.0 copy-done.2
  68.6 1.3 %soap_step.1 = (f32[64,64]{1,0:T(8,128)}, f32[64,64]{1,0:T(8,128)}, f32[64,64]{1,0:T(8,128)}) custom-call(f32[8,32,128]{2,1,0:T(8,128)S(1)} %all_to_all.17.parts_ref, f32[64,64]{1,0:T(8,128)S(1)} %bitcast.18, f32[64,64]{1,0:T(8,128)S(1)} %bitcast.19, f32[64,64]{1,0:T(8,128)S(1)} %bitcast.20, f32[64,64]{1,0:T(8,128)S(1)} %bitcast.21, f32[64,64]{1,0:T(8,128)S(1)} %bitcast.22), custom_call_target="tpu_custom_call" | custom-call | tf_op jit(solution)/shard_map/soap_step/pallas_call | solution.py:75
  (3 shorter events, 0.0 us)
Async XLA Ops:
  0.6 22.5 %copy-start.6 = (bf16[1024,512]{1,0:T(8,128)(2,1)S(1)}, bf16[1024,512]{1,0:T(8,128)(2,1)}, u32[]{:S(2)}) copy-start(bf16[1024,512]{1,0:T(8,128)(2,1)} %param.8) | copy-start | bytes 3145732
  21.2 4.5 %collective-permute-start = (bf16[512,1024]{1,0:T(8,128)(2,1)S(1)}, bf16[512,1024]{1,0:T(8,128)(2,1)S(1)}, u32[]{:S(2)}, u32[]{:S(2)}) collective-permute-start(bf16[512,1024]{1,0:T(8,128)(2,1)S(1)} %bitcast.24), channel_id=1, source_target_pairs={{0,1},{1,0},{2,3},{3,2},{4,5},{5,4},{6,7},{7,6},{8,9},{9,8},{10,11... | collective-permute-start | bytes 3145736 | tf_op jit(solution)/shard_map/ppermute | solution.py:97
  25.7 0.8 %copy-start.5 = (s32[64,8]{0,1:T(8,128)S(1)}, s32[64,8]{0,1:T(8,128)}, u32[]{:S(2)}) copy-start(s32[64,8]{0,1:T(8,128)} %param.10) | copy-start | bytes 6148
  27.3 41.3 %copy-start = (f32[1,1,1,64,64]{4,3,2,1,0:T(8,128)S(1)}, f32[1,1,1,64,64]{4,3,2,1,0:T(8,128)}, u32[]{:S(2)}) copy-start(f32[1,1,1,64,64]{4,3,2,1,0:T(8,128)} %param.11) | copy-start | bytes 49156
  27.3 41.3 %copy-start.1 = (f32[1,1,1,64,64]{4,3,2,1,0:T(8,128)S(1)}, f32[1,1,1,64,64]{4,3,2,1,0:T(8,128)}, u32[]{:S(2)}) copy-start(f32[1,1,1,64,64]{4,3,2,1,0:T(8,128)} %param.12) | copy-start | bytes 49156
  27.3 41.3 %copy-start.2 = (f32[1,1,1,64,64]{4,3,2,1,0:T(8,128)S(1)}, f32[1,1,1,64,64]{4,3,2,1,0:T(8,128)}, u32[]{:S(2)}) copy-start(f32[1,1,1,64,64]{4,3,2,1,0:T(8,128)} %param.13) | copy-start | bytes 49156
  27.3 41.3 %copy-start.3 = (f32[1,1,1,64,64]{4,3,2,1,0:T(8,128)S(1)}, f32[1,1,1,64,64]{4,3,2,1,0:T(8,128)}, u32[]{:S(2)}) copy-start(f32[1,1,1,64,64]{4,3,2,1,0:T(8,128)} %param.14) | copy-start | bytes 49156
  27.3 41.3 %copy-start.4 = (f32[1,1,1,64,64]{4,3,2,1,0:T(8,128)S(1)}, f32[1,1,1,64,64]{4,3,2,1,0:T(8,128)}, u32[]{:S(2)}) copy-start(f32[1,1,1,64,64]{4,3,2,1,0:T(8,128)} %param.15) | copy-start | bytes 49156

commit v5 on v4

--- a/solution.py
+++ b/solution.py
@@ -16,16 +16,11 @@
 
 
 def pack_kernel(keep_ref, grad_ref, out_ref):
-    seq = lax.axis_index("y") * lax.axis_size("c") + lax.axis_index("c")
     share_blocks = grad_ref.shape[0] // BLOCK
     left = lax.broadcasted_iota(jnp.int32, (HALF, LANES), 1) < BLOCK
-    keep = keep_ref[...]
-    coded = keep << (4 * lax.broadcasted_iota(jnp.int32, keep.shape, 0))
-    block = lax.broadcasted_iota(jnp.int32, keep.shape, 1) - seq * share_blocks
-    codes = [jnp.sum(jnp.where(block == r, coded, 0)) for r in range(share_blocks)]
-    for r, code in enumerate(codes):
+    for r in range(share_blocks):
         for k in range(keep_ref.shape[0]):
-            col = (code >> (4 * k)) & 15
+            col = keep_ref[k, r]
             lanes = pl.ds(pl.multiple_of((col // 2) * LANES, LANES), LANES)
             odd = (col % 2) == 1
             top = grad_ref[r * BLOCK : r * BLOCK + HALF, lanes]
@@ -40,15 +35,35 @@
     return pltpu.with_memory_space_constraint(x, pltpu.VMEM)
 
 
+def share_kernel(keep_ref, out_ref):
+    seq = lax.axis_index("y") * lax.axis_size("c") + lax.axis_index("c")
+    for k in range(out_ref.shape[0]):
+        for r in range(out_ref.shape[1]):
+            out_ref[k, r] = keep_ref[k, seq * out_ref.shape[1] + r]
+
+
+def kept_share(keep, share_blocks):
+    return pl.pallas_call(
+        share_kernel,
+        out_shape=pltpu.SMEM((keep.shape[0], share_blocks), keep.dtype),
+        in_specs=[pl.BlockSpec(memory_space=pltpu.SMEM)],
+        out_specs=pl.BlockSpec(memory_space=pltpu.SMEM),
+        name="kept_share",
+    )(keep)
+
+
 def pack_kept(keep, grad):
     kept = keep.shape[0]
     return pl.pallas_call(
         pack_kernel,
         out_shape=pltpu.VMEM((kept, grad.shape[0] // 2, LANES), jnp.float32),
-        in_specs=[pl.BlockSpec(memory_space=pltpu.VMEM)] * 2,
+        in_specs=[
+            pl.BlockSpec(memory_space=pltpu.SMEM),
+            pl.BlockSpec(memory_space=pltpu.VMEM),
+        ],
         out_specs=pl.BlockSpec(memory_space=pltpu.VMEM),
         name="pack_kept",
-    )(pin(keep), pin(grad))
+    )(pltpu.with_memory_space_constraint(keep, pltpu.SMEM), pin(grad))
 
 
 def dot(a, b, ca, cb):
@@ -109,7 +124,7 @@
         )
 
     grad = term(mine, own) + term(1 - mine, other)
-    packed = pack_kept(keep_lists.T, grad)
+    packed = pack_kept(kept_share(keep_lists.T, acts.shape[1] // BLOCK), grad)
     near = exchange((packed * SCALE).astype(jnp.float16), ("zl", "x"))
     summed = jnp.sum(near.astype(jnp.float32), axis=0).reshape(-1, HALF, LANES)
     parts = exchange(summed, "zh", FAR_ORDER)

time: 70.9 us -> 70.7 us (level)
  waiting for transfers between devices: 1.8 us -> 0.94 us
    ppermute x1, waiting for transfers between devices: 1.8 us -> 0.94 us  [per_device(): other = lax.ppermute(own, 'c', [(0, 1), (1, 0)])]
    pallas_call x0 -> x1, Pallas kernels: none -> 0.84 us  [kept_share(): pl.pallas_call(share_kernel, out_shape=pltpu.SMEM((keep.shape[0], share_b...]
  transfers between devices with their start and end apart: 1 -> 1, of which waited for: 1 -> 1; matrix products, arithmetic and copies ran while one was open for 1% -> 1% of each run, Pallas kernels for 0% -> 1%
where the time goes in v5:
time: 70.7 us; the launch traced here: 69.8 us
  blocking collectives  60.4 us (85%)
  Pallas kernels  2.8 us (4%)
  starting transfers between devices  1.91 us (3%)
  matrix products  1.46 us (2%)
  local copies, waits for them, and re-layouts  1.27 us (2%)
  waiting for transfers between devices  0.94 us (1%)
  between operations  0.77 us (1%)
    all_to_all x3, blocking collectives, exchange(): lax.all_to_all(x, axes, split_axis=0, concat_axis=0, tiled=True, axis_ind...  60.4 us
    ppermute x1, starting transfers between devices, per_device(): other = lax.ppermute(own, 'c', [(0, 1), (1, 0)])  1.91 us
    dot_general x2, matrix products, term(): lax.dot_general(half.reshape(ny * tokens, feats), rows, (((0,), (0,)), ((...  1.46 us
  transfers between devices with their start and end apart: 1, of which 1 were waited for; matrix products, arithmetic and copies ran while one was open for 1% of the time, Pallas kernels for 1%

profile of v5, /device:TPU:6, one launch (start us, length us, event | category | flops | bytes accessed | tf_op | source)
XLA Modules:
  0.0 69.8 jit_solution(8989360206905701543)
XLA Ops:
  0.6 0.0 copy-start.5
  0.6 1.2 %broadcast_in_dim.2 = bf16[4,128,1024]{2,1,0:T(8,128)(2,1)S(1)} broadcast(bf16[128,1024]{1,0:T(8,128)(2,1)} %param.9), dimensions={1,2} | broadcast | bytes 1310720 | tf_op jit(solution)/shard_map/broadcast_in_dim | solution.py:109
  1.8 19.4 %all_to_all.15 = bf16[4,128,1024]{2,1,0:T(8,128)(2,1)S(1)} all-to-all(bf16[4,128,1024]{2,1,0:T(8,128)(2,1)S(1)} %broadcast_in_dim.2), channel_id=1, replica_groups=mesh['zh'=8,'zl'=2,'x'=4,'y'=4,'c'=2] {'y'}, dimensions={0} | all-to-all | bytes 2097152 | tf_op jit(solution)/shard_map/all_to_all | solution.py:101
  21.2 1.9 %collective-permute-start = (bf16[512,1024]{1,0:T(8,128)(2,1)S(1)}, bf16[512,1024]{1,0:T(8,128)(2,1)S(1)}, u32[]{:S(2)}, u32[]{:S(2)}) collective-permute-start(bf16[512,1024]{1,0:T(8,128)(2,1)S(1)} %bitcast.23), channel_id=1, source_target_pairs={{0,1},{1,0},{2,3},{3,2},{4,5},{5,4},{6,7},{7,6},{8,9},{9,8},{10,11... | collective-permute-start | bytes 3145736 | tf_op jit(solution)/shard_map/ppermute | solution.py:112
  23.1 0.8 %kept_share.1.keep_ref = s32[8,8]{1,0:T(8,128)S(4)} custom-call(s32[8,64]{1,0:T(8,128)} %bitcast.29), custom_call_target="tpu_custom_call" | custom-call | tf_op jit(solution)/shard_map/kept_share/pallas_call | solution.py:46
  23.9 0.0 copy-done.5
  23.9 0.1 constant_dynamic-slice_fusion
  24.0 0.7 %fusion = f32[512,1024]{1,0:T(8,128)S(1)} fusion(bf16[512,512]{1,0:T(8,128)(2,1)S(1)} %bitcast.25, bf16[512,1024]{1,0:T(8,128)(2,1)S(1)} %bitcast.24), kind=kOutput, calls=%fused_computation.5 | convolution fusion | flops 536870912 | bytes 3670016 | tf_op jit(solution)/shard_map/dot_general | solution.py:119
  24.8 0.9 %collective-permute-done = bf16[512,1024]{1,0:T(8,128)(2,1)S(1)} collective-permute-done((bf16[512,1024]{1,0:T(8,128)(2,1)S(1)}, bf16[512,1024]{1,0:T(8,128)(2,1)S(1)}, u32[]{:S(2)}, u32[]{:S(2)}) %collective-permute-start) | collective-permute-done | bytes 1048608 | tf_op jit(solution)/shard_map/ppermute | solution.py:112
  25.7 0.7 %convolution_add_fusion.grad_ref = f32[512,1024]{1,0:T(8,128)S(1)} fusion(f32[512,1024]{1,0:T(8,128)S(1)} %fusion, bf16[512,512]{1,0:T(8,128)(2,1)S(1)} %bitcast.26, bf16[512,1024]{1,0:T(8,128)(2,1)S(1)} %collective-permute-done), kind=kOutput, calls=%fused_computation | convolution fusion | flops 537395200 | bytes 5767168 | tf_op jit(solution)/shard_map/dot_general | solution.py:119
  26.4 0.6 pack_kept.1
  27.1 0.0 copy-start
  27.1 0.0 copy-start.1
  27.1 0.0 copy-start.2
  27.1 0.0 copy-start.3
  27.1 0.0 copy-start.4
  27.1 0.1 multiply_convert_fusion
  27.2 13.8 %all_to_all.16 = f16[8,256,128]{2,1,0:T(8,128)(2,1)S(1)} all-to-all(f16[8,256,128]{2,1,0:T(8,128)(2,1)S(1)} %multiply_convert_fusion), channel_id=1, replica_groups=mesh['zh'=8,'zl'=2,'x'=4,'y'=4,'c'=2] {'zl','x'}, dimensions={0} | all-to-all | bytes 1048576 | tf_op jit(solution)/shard_map/all_to_all | solution.py:101
  41.1 0.1 convert_reduce_fusion
  41.1 27.2 %all_to_all.17.parts_ref = f32[8,32,128]{2,1,0:T(8,128)S(1)} all-to-all(f32[8,32,128]{2,1,0:T(8,128)S(1)} %bitcast.28), channel_id=1, replica_groups={{0,256,128,384,64,320,192,448},{1,257,129,385,65,321,193,449},{2,258,13..., dimensions={0} | all-to-all | bytes 262144 | tf_op jit(solution)/shard_map/all_to_all | solution.py:101
  68.4 0.0 copy-done
  68.4 0.0 copy-done.1
  68.4 0.0 copy-done.2
  68.4 1.3 %soap_step.1 = (f32[64,64]{1,0:T(8,128)}, f32[64,64]{1,0:T(8,128)}, f32[64,64]{1,0:T(8,128)}) custom-call(f32[8,32,128]{2,1,0:T(8,128)S(1)} %all_to_all.17.parts_ref, f32[64,64]{1,0:T(8,128)S(1)} %bitcast.18, f32[64,64]{1,0:T(8,128)S(1)} %bitcast.19, f32[64,64]{1,0:T(8,128)S(1)} %bitcast.20, f32[64,64]{1,0:T(8,128)S(1)} %bitcast.21, f32[64,64]{1,0:T(8,128)S(1)} %bitcast.22), custom_call_target="tpu_custom_call" | custom-call | tf_op jit(solution)/shard_map/soap_step/pallas_call | solution.py:90
  (2 shorter events, 0.0 us)
Async XLA Ops:
  0.6 23.3 %copy-start.5 = (bf16[1024,512]{1,0:T(8,128)(2,1)S(1)}, bf16[1024,512]{1,0:T(8,128)(2,1)}, u32[]{:S(2)}) copy-start(bf16[1024,512]{1,0:T(8,128)(2,1)} %param.8) | copy-start | bytes 3145732
  21.2 4.5 %collective-permute-start = (bf16[512,1024]{1,0:T(8,128)(2,1)S(1)}, bf16[512,1024]{1,0:T(8,128)(2,1)S(1)}, u32[]{:S(2)}, u32[]{:S(2)}) collective-permute-start(bf16[512,1024]{1,0:T(8,128)(2,1)S(1)} %bitcast.23), channel_id=1, source_target_pairs={{0,1},{1,0},{2,3},{3,2},{4,5},{5,4},{6,7},{7,6},{8,9},{9,8},{10,11... | collective-permute-start | bytes 3145736 | tf_op jit(solution)/shard_map/ppermute | solution.py:112
  27.1 41.3 %copy-start = (f32[1,1,1,64,64]{4,3,2,1,0:T(8,128)S(1)}, f32[1,1,1,64,64]{4,3,2,1,0:T(8,128)}, u32[]{:S(2)}) copy-start(f32[1,1,1,64,64]{4,3,2,1,0:T(8,128)} %param.11) | copy-start | bytes 49156
  27.1 41.3 %copy-start.1 = (f32[1,1,1,64,64]{4,3,2,1,0:T(8,128)S(1)}, f32[1,1,1,64,64]{4,3,2,1,0:T(8,128)}, u32[]{:S(2)}) copy-start(f32[1,1,1,64,64]{4,3,2,1,0:T(8,128)} %param.12) | copy-start | bytes 49156
  27.1 41.3 %copy-start.2 = (f32[1,1,1,64,64]{4,3,2,1,0:T(8,128)S(1)}, f32[1,1,1,64,64]{4,3,2,1,0:T(8,128)}, u32[]{:S(2)}) copy-start(f32[1,1,1,64,64]{4,3,2,1,0:T(8,128)} %param.13) | copy-start | bytes 49156
  27.1 41.3 %copy-start.3 = (f32[1,1,1,64,64]{4,3,2,1,0:T(8,128)S(1)}, f32[1,1,1,64,64]{4,3,2,1,0:T(8,128)}, u32[]{:S(2)}) copy-start(f32[1,1,1,64,64]{4,3,2,1,0:T(8,128)} %param.14) | copy-start | bytes 49156
  27.1 41.3 %copy-start.4 = (f32[1,1,1,64,64]{4,3,2,1,0:T(8,128)S(1)}, f32[1,1,1,64,64]{4,3,2,1,0:T(8,128)}, u32[]{:S(2)}) copy-start(f32[1,1,1,64,64]{4,3,2,1,0:T(8,128)} %param.15) | copy-start | bytes 49156

commit v6 on v5

--- a/solution.py
+++ b/solution.py
@@ -11,6 +11,7 @@
 DATA = ("zh", "zl", "x")
 SEQ = ("y", "c")
 SCALE = 1024.0
+RING_ORDER = (0, 1, 3, 2)
 FAR_ORDER = (0, 4, 2, 6, 1, 5, 3, 7)
 PRECISION = lax.Precision.HIGH
 
@@ -107,12 +108,13 @@
     tokens, cols = upstream.shape
     ny = lax.axis_size("y")
     spread = jnp.broadcast_to(upstream[None], (ny, tokens, cols))
-    own = exchange(spread, "y")
+    own = exchange(spread, "y", RING_ORDER)
     own = own.reshape(ny * tokens, cols)
     other = lax.ppermute(own, "c", [(0, 1), (1, 0)])
     mine = lax.axis_index("c")
     feats = acts.shape[1]
     halves = acts.reshape(ny, 2, tokens, feats)
+    halves = jnp.stack([halves[chip] for chip in RING_ORDER])
 
     def term(core, rows):
         half = lax.dynamic_index_in_dim(halves, core, 1, keepdims=False)

time: 70.7 us -> 70.5 us (level)
  no operation moved by 1% of the time
where the time goes in v6:
time: 70.5 us; the launch traced here: 69.5 us
  blocking collectives  60.1 us (85%)
  Pallas kernels  2.8 us (4%)
  starting transfers between devices  1.91 us (3%)
  matrix products  1.45 us (2%)
  local copies, waits for them, and re-layouts  1.34 us (2%)
  between operations  0.78 us (1%)
  waiting for transfers between devices  0.73 us (1%)
    all_to_all x3, blocking collectives, exchange(): lax.all_to_all(x, axes, split_axis=0, concat_axis=0, tiled=True, axis_ind...  60.1 us
    ppermute x1, starting transfers between devices, per_device(): other = lax.ppermute(own, 'c', [(0, 1), (1, 0)])  1.91 us
    dot_general x2, matrix products, term(): lax.dot_general(half.reshape(ny * tokens, feats), rows, (((0,), (0,)), ((...  1.45 us
  transfers between devices with their start and end apart: 1, of which 1 were waited for; matrix products, arithmetic and copies ran while one was open for 1% of the time, Pallas kernels for 1%

profile of v6, /device:TPU:6, one launch (start us, length us, event | category | flops | bytes accessed | tf_op | source)
XLA Modules:
  0.0 69.5 jit_solution(12532161970901552070)
XLA Ops:
  0.6 0.0 copy-start.5
  0.6 1.2 %broadcast_in_dim.2 = bf16[4,128,1024]{2,1,0:T(8,128)(2,1)S(1)} broadcast(bf16[128,1024]{1,0:T(8,128)(2,1)} %param.9), dimensions={1,2} | broadcast | bytes 1310720 | tf_op jit(solution)/shard_map/broadcast_in_dim | solution.py:110
  1.8 19.1 %all_to_all.15 = bf16[4,128,1024]{2,1,0:T(8,128)(2,1)S(1)} all-to-all(bf16[4,128,1024]{2,1,0:T(8,128)(2,1)S(1)} %broadcast_in_dim.2), channel_id=1, replica_groups={{0,2,6,4},{1,3,7,5},{8,10,14,12},{9,11,15,13},{16,18,22,20},{17,19,23,2..., dimensions={0} | all-to-all | bytes 2097152 | tf_op jit(solution)/shard_map/all_to_all | solution.py:102
  20.9 1.9 %collective-permute-start = (bf16[512,1024]{1,0:T(8,128)(2,1)S(1)}, bf16[512,1024]{1,0:T(8,128)(2,1)S(1)}, u32[]{:S(2)}, u32[]{:S(2)}) collective-permute-start(bf16[512,1024]{1,0:T(8,128)(2,1)S(1)} %bitcast.26), channel_id=1, source_target_pairs={{0,1},{1,0},{2,3},{3,2},{4,5},{5,4},{6,7},{7,6},{8,9},{9,8},{10,11... | collective-permute-start | bytes 3145736 | tf_op jit(solution)/shard_map/ppermute | solution.py:113
  22.8 0.8 %kept_share.1.keep_ref = s32[8,8]{1,0:T(8,128)S(4)} custom-call(s32[8,64]{1,0:T(8,128)} %bitcast.35), custom_call_target="tpu_custom_call" | custom-call | tf_op jit(solution)/shard_map/kept_share/pallas_call | solution.py:47
  23.6 0.0 copy-done.5
  23.6 0.1 fusion
  23.7 0.1 pad_maximum_fusion
  23.9 0.1 constant_dynamic-slice_fusion
  24.0 0.7 %fusion.1 = f32[512,1024]{1,0:T(8,128)S(1)} fusion(bf16[512,512]{1,0:T(8,128)(2,1)S(1)} %bitcast.28, bf16[512,1024]{1,0:T(8,128)(2,1)S(1)} %bitcast.27), kind=kOutput, calls=%fused_computation.7 | convolution fusion | flops 536870912 | bytes 3670016 | tf_op jit(solution)/shard_map/dot_general | solution.py:121
  24.7 0.7 %collective-permute-done = bf16[512,1024]{1,0:T(8,128)(2,1)S(1)} collective-permute-done((bf16[512,1024]{1,0:T(8,128)(2,1)S(1)}, bf16[512,1024]{1,0:T(8,128)(2,1)S(1)}, u32[]{:S(2)}, u32[]{:S(2)}) %collective-permute-start) | collective-permute-done | bytes 1048608 | tf_op jit(solution)/shard_map/ppermute | solution.py:113
  25.4 0.7 %convolution_add_fusion.grad_ref = f32[512,1024]{1,0:T(8,128)S(1)} fusion(f32[512,1024]{1,0:T(8,128)S(1)} %fusion.1, bf16[512,512]{1,0:T(8,128)(2,1)S(1)} %bitcast.29, bf16[512,1024]{1,0:T(8,128)(2,1)S(1)} %collective-permute-done), kind=kOutput, calls=%fused_computation | convolution fusion | flops 537395200 | bytes 5767168 | tf_op jit(solution)/shard_map/dot_general | solution.py:121
  26.1 0.6 pack_kept.1
  26.8 0.0 copy-start
  26.8 0.0 copy-start.1
  26.8 0.0 copy-start.2
  26.8 0.0 copy-start.3
  26.8 0.0 copy-start.4
  26.8 0.1 multiply_convert_fusion
  26.9 13.8 %all_to_all.16 = f16[8,256,128]{2,1,0:T(8,128)(2,1)S(1)} all-to-all(f16[8,256,128]{2,1,0:T(8,128)(2,1)S(1)} %multiply_convert_fusion), channel_id=1, replica_groups=mesh['zh'=8,'zl'=2,'x'=4,'y'=4,'c'=2] {'zl','x'}, dimensions={0} | all-to-all | bytes 1048576 | tf_op jit(solution)/shard_map/all_to_all | solution.py:102
  40.8 0.1 convert_reduce_fusion
  40.9 27.2 %all_to_all.17.parts_ref = f32[8,32,128]{2,1,0:T(8,128)S(1)} all-to-all(f32[8,32,128]{2,1,0:T(8,128)S(1)} %bitcast.34), channel_id=1, replica_groups={{0,256,128,384,64,320,192,448},{1,257,129,385,65,321,193,449},{2,258,13..., dimensions={0} | all-to-all | bytes 262144 | tf_op jit(solution)/shard_map/all_to_all | solution.py:102
  68.1 0.0 copy-done
  68.1 1.3 %soap_step.1 = (f32[64,64]{1,0:T(8,128)}, f32[64,64]{1,0:T(8,128)}, f32[64,64]{1,0:T(8,128)}) custom-call(f32[8,32,128]{2,1,0:T(8,128)S(1)} %all_to_all.17.parts_ref, f32[64,64]{1,0:T(8,128)S(1)} %bitcast.21, f32[64,64]{1,0:T(8,128)S(1)} %bitcast.22, f32[64,64]{1,0:T(8,128)S(1)} %bitcast.23, f32[64,64]{1,0:T(8,128)S(1)} %bitcast.24, f32[64,64]{1,0:T(8,128)S(1)} %bitcast.25), custom_call_target="tpu_custom_call" | custom-call | tf_op jit(solution)/shard_map/soap_step/pallas_call | solution.py:91
  (4 shorter events, 0.0 us)
Async XLA Ops:
  0.6 23.0 %copy-start.5 = (bf16[1024,512]{1,0:T(8,128)(2,1)S(1)}, bf16[1024,512]{1,0:T(8,128)(2,1)}, u32[]{:S(2)}) copy-start(bf16[1024,512]{1,0:T(8,128)(2,1)} %param.8) | copy-start | bytes 3145732
  20.9 4.5 %collective-permute-start = (bf16[512,1024]{1,0:T(8,128)(2,1)S(1)}, bf16[512,1024]{1,0:T(8,128)(2,1)S(1)}, u32[]{:S(2)}, u32[]{:S(2)}) collective-permute-start(bf16[512,1024]{1,0:T(8,128)(2,1)S(1)} %bitcast.26), channel_id=1, source_target_pairs={{0,1},{1,0},{2,3},{3,2},{4,5},{5,4},{6,7},{7,6},{8,9},{9,8},{10,11... | collective-permute-start | bytes 3145736 | tf_op jit(solution)/shard_map/ppermute | solution.py:113
  26.8 41.3 %copy-start = (f32[1,1,1,64,64]{4,3,2,1,0:T(8,128)S(1)}, f32[1,1,1,64,64]{4,3,2,1,0:T(8,128)}, u32[]{:S(2)}) copy-start(f32[1,1,1,64,64]{4,3,2,1,0:T(8,128)} %param.11) | copy-start | bytes 49156
  26.8 41.3 %copy-start.1 = (f32[1,1,1,64,64]{4,3,2,1,0:T(8,128)S(1)}, f32[1,1,1,64,64]{4,3,2,1,0:T(8,128)}, u32[]{:S(2)}) copy-start(f32[1,1,1,64,64]{4,3,2,1,0:T(8,128)} %param.12) | copy-start | bytes 49156
  26.8 41.3 %copy-start.2 = (f32[1,1,1,64,64]{4,3,2,1,0:T(8,128)S(1)}, f32[1,1,1,64,64]{4,3,2,1,0:T(8,128)}, u32[]{:S(2)}) copy-start(f32[1,1,1,64,64]{4,3,2,1,0:T(8,128)} %param.13) | copy-start | bytes 49156
  26.8 41.3 %copy-start.3 = (f32[1,1,1,64,64]{4,3,2,1,0:T(8,128)S(1)}, f32[1,1,1,64,64]{4,3,2,1,0:T(8,128)}, u32[]{:S(2)}) copy-start(f32[1,1,1,64,64]{4,3,2,1,0:T(8,128)} %param.14) | copy-start | bytes 49156
  26.8 41.3 %copy-start.4 = (f32[1,1,1,64,64]{4,3,2,1,0:T(8,128)S(1)}, f32[1,1,1,64,64]{4,3,2,1,0:T(8,128)}, u32[]{:S(2)}) copy-start(f32[1,1,1,64,64]{4,3,2,1,0:T(8,128)} %param.15) | copy-start | bytes 49156
